TPU v7x, 512 devices: a whole 4x8x8 slice. The times are simulated.
512 devices in a mesh: seq: 128 (over z, y, core), head: 4 (over x).
Axes of the slice: x: 4, y: 8, z: 8, core: 2. Of those that a mesh axis runs over, the one named last changes fastest.
Arguments:
- queries: bfloat16 [32768, 4096], P('seq', 'head'), may hold values from -6 to 6
- keys: bfloat16 [32768, 512], P(('seq', 'head')), may hold values from -6 to 6
- values: bfloat16 [32768, 512], P(('seq', 'head')), may hold values from -6 to 6
- d_out: bfloat16 [32768, 4096], P('seq', 'head'), may hold values from -6 to 6
- rand_blocks: int32 [512, 8], P('seq'), may hold values from 0 to 511, as said below
- glob_blocks: int32 [2], replicated, may hold values from 0 to 511
Outputs:
- attn_out: bfloat16 [32768, 4096], P('seq', 'head')
- d_queries: bfloat16 [32768, 4096], P('seq', 'head')
- d_keys: bfloat16 [32768, 512], P(('seq', 'head'))
- d_values: bfloat16 [32768, 512], P(('seq', 'head'))
Inputs may be any that keep to these rules, and one draw needn't show every extreme that they name: `rand_blocks`: block b lies on index b // 4 of seq. Among the 32 entries of the query blocks of one index of seq, at most 1 name blocks of any one index, and some index of seq reaches 1 for some owner in every draw.
All inputs are finite; a program needn't handle non-finite values.
Results may differ from a plain program's by a relative error of at most 0.012.
Values may be sent and summed in bfloat16 or wider, within the bound.
A program may use at most 64 MiB of HBM per device.

v0:
```python
import jax
import jax.numpy as jnp
from jax import lax
from jax.sharding import PartitionSpec as P

DH = 128
KVH = 4
BLOCK = 64
GLOB = 2
RAND = 8
NEG_FILL = -1e30


def padded_2(cells, sides, width):
    for axis, dim in sides:
        count = lax.axis_size(axis)
        ends = count - 1
        head = lax.slice_in_dim(cells, 0, width, axis=dim)
        tail = lax.slice_in_dim(cells, cells.shape[dim] - width, cells.shape[dim], axis=dim)
        cells = jnp.concatenate(
            [
                lax.ppermute(tail, axis, [(i, (i + 1) % count) for i in range(ends)]),
                cells,
                lax.ppermute(head, axis, [((i + 1) % count, i) for i in range(ends)]),
            ],
            axis=dim,
        )
    return cells


def broadcast(block, axis, source):
    block = jnp.where(lax.axis_index(axis) == source, block, jnp.zeros_like(block))
    return lax.psum(block, axis)


def key_rows(library, spots):
    chosen = library[spots]
    flat = chosen.reshape(chosen.shape[0] * chosen.shape[1], chosen.shape[2])
    return (flat[:, :DH], flat[:, DH:])


def masked_scores(query_block, keys_here, allowed_row):
    factor = DH ** (-0.5)
    scores = (
        jnp.einsum("thd,kd->htk", query_block, keys_here, preferred_element_type=jnp.float32)
        * factor
    )
    widened = jnp.repeat(allowed_row, keys_here.shape[0] // allowed_row.shape[0])
    return jnp.where(widened[None, None, :], scores, NEG_FILL)


def body(queries, keys, values, d_out, rand_blocks, glob_blocks):
    seq_count = lax.axis_size("seq")
    here = lax.axis_index("seq")
    short = keys.shape[0]
    stacked = jnp.concatenate(
        [keys.reshape(short, KVH, DH), values.reshape(short, KVH, DH)], axis=2
    )
    mine = lax.all_to_all(stacked, "head", split_axis=1, concat_axis=0, tiled=True)
    tok_count = mine.shape[0]
    blocks_here = tok_count // BLOCK
    flat_pairs = mine.reshape(tok_count, 2 * DH)
    own_blocks = flat_pairs.reshape(blocks_here, BLOCK, 2 * DH)
    padded = padded_2(flat_pairs, (("seq", 0),), BLOCK)
    window = padded.reshape(blocks_here + 2, BLOCK, 2 * DH)
    global_parts = []
    for number in range(GLOB):
        target = glob_blocks[number]
        piece = lax.dynamic_index_in_dim(own_blocks, target % blocks_here, 0, keepdims=False)
        global_parts.append(broadcast(piece, "seq", target // blocks_here))
    global_pairs = jnp.stack(global_parts)
    entries = rand_blocks.reshape(-1)
    entry_count = entries.shape[0]
    capacity = -(-entry_count // seq_count)
    position_count = seq_count * capacity
    owners = entries // blocks_here
    inner_index = entries % blocks_here
    order = jnp.arange(entry_count, dtype=jnp.int32)
    earlier = (owners[:, None] == owners[None, :]) & (order[:, None] > order[None, :])
    ranks = jnp.sum(earlier.astype(jnp.int32), axis=1)
    slots = owners * capacity + ranks
    placing = slots[None, :] == jnp.arange(position_count, dtype=jnp.int32)[:, None]
    wanted = jnp.sum(jnp.where(placing, inner_index[None, :], 0), axis=1).reshape(
        seq_count, capacity
    )
    incoming = lax.all_to_all(wanted, "seq", split_axis=0, concat_axis=0, tiled=True).reshape(
        position_count
    )
    served = own_blocks[incoming].reshape(seq_count, capacity, BLOCK, 2 * DH)
    fetched = lax.all_to_all(served, "seq", split_axis=0, concat_axis=0, tiled=True).reshape(
        position_count, BLOCK, 2 * DH
    )
    block_ids = jnp.arange(blocks_here, dtype=jnp.int32)
    window_ids = jnp.stack([block_ids, block_ids + 1, block_ids + 2], axis=1)
    global_ids = jnp.broadcast_to(
        blocks_here + 2 + jnp.arange(GLOB, dtype=jnp.int32), (blocks_here, GLOB)
    )
    random_ids = blocks_here + 2 + GLOB + slots.reshape(blocks_here, RAND)
    positions = jnp.concatenate([window_ids, global_ids, random_ids], axis=1)
    allowed = jnp.concatenate(
        [
            jnp.logical_not((block_ids == 0) & (here == 0))[:, None],
            jnp.ones((blocks_here, 1), jnp.bool_),
            jnp.logical_not((block_ids == blocks_here - 1) & (here == seq_count - 1))[:, None],
            jnp.ones((blocks_here, GLOB + RAND), jnp.bool_),
        ],
        axis=1,
    )
    library = jnp.concatenate([window, global_pairs, fetched], axis=0)
    heads_here = queries.shape[1] // DH
    query_blocks = queries.reshape(blocks_here, BLOCK, heads_here, DH)
    grad_blocks = d_out.reshape(blocks_here, BLOCK, heads_here, DH)

    def forward_step(inputs):
        query_block, spots, allowed_row = inputs
        keys_here, values_here = key_rows(library, spots)
        scores = masked_scores(query_block, keys_here, allowed_row)
        peak = jnp.max(scores, axis=-1, keepdims=True)
        logsum = peak + jnp.log(jnp.sum(jnp.exp(scores - peak), axis=-1, keepdims=True))
        probs16 = jnp.exp(scores - logsum).astype(jnp.bfloat16)
        result = jnp.einsum("htk,kd->thd", probs16, values_here, preferred_element_type=jnp.float32)
        return (result.astype(jnp.bfloat16), logsum)

    out_blocks, logsums = lax.map(forward_step, (query_blocks, positions, allowed))
    refetched = lax.all_to_all(served, "seq", split_axis=0, concat_axis=0, tiled=True).reshape(
        position_count, BLOCK, 2 * DH
    )
    library_back = jnp.concatenate([window, global_pairs, refetched], axis=0)

    def backward_step(inputs):
        query_block, gradient_tile, out_block, logsum, spots, allowed_row = inputs
        keys_here, values_here = key_rows(library_back, spots)
        factor = DH ** (-0.5)
        scores = masked_scores(query_block, keys_here, allowed_row)
        probs = jnp.exp(scores - logsum)
        probs16 = probs.astype(jnp.bfloat16)
        delta = jnp.sum(gradient_tile.astype(jnp.float32) * out_block.astype(jnp.float32), axis=-1)
        dprobs = jnp.einsum(
            "thd,kd->htk", gradient_tile, values_here, preferred_element_type=jnp.float32
        )
        dscores = (probs * (dprobs - jnp.transpose(delta)[:, :, None])).astype(jnp.bfloat16)
        dquery = (
            jnp.einsum("htk,kd->thd", dscores, keys_here, preferred_element_type=jnp.float32)
            * factor
        )
        dkey = (
            jnp.einsum("htk,thd->kd", dscores, query_block, preferred_element_type=jnp.float32)
            * factor
        )
        dvalue = jnp.einsum(
            "htk,thd->kd", probs16, gradient_tile, preferred_element_type=jnp.float32
        )
        terms = jnp.concatenate([dkey, dvalue], axis=1).reshape(spots.shape[0], BLOCK, 2 * DH)
        return (dquery.astype(jnp.bfloat16), terms)

    dquery_blocks, terms = lax.map(
        backward_step, (query_blocks, grad_blocks, out_blocks, logsums, positions, allowed)
    )
    attn_out = out_blocks.reshape(tok_count, heads_here * DH)
    d_queries = dquery_blocks.reshape(tok_count, heads_here * DH)
    prev_terms = terms[:, 0]
    self_terms = terms[:, 1]
    next_terms = terms[:, 2]
    zero_block = jnp.zeros((1, BLOCK, 2 * DH), jnp.float32)
    grads = (
        self_terms
        + jnp.concatenate([prev_terms[1:], zero_block], axis=0)
        + jnp.concatenate([zero_block, next_terms[:-1]], axis=0)
    )
    rims = jnp.concatenate([prev_terms[0], next_terms[-1]], axis=0).astype(jnp.bfloat16)
    arrived = padded_2(rims, (("seq", 0),), BLOCK)
    from_left = arrived[:BLOCK].astype(jnp.float32)
    from_right = arrived[3 * BLOCK :].astype(jnp.float32)
    edge_first = jnp.concatenate(
        [from_left[None], jnp.zeros((blocks_here - 1, BLOCK, 2 * DH), jnp.float32)], axis=0
    )
    edge_last = jnp.concatenate(
        [jnp.zeros((blocks_here - 1, BLOCK, 2 * DH), jnp.float32), from_right[None]], axis=0
    )
    grads = grads + edge_first + edge_last
    global_terms = jnp.sum(terms[:, 3 : 3 + GLOB], axis=0)
    global_total = lax.psum(global_terms, "seq")
    global_hits = ((glob_blocks // blocks_here)[:, None] == here) & (
        (glob_blocks % blocks_here)[:, None] == block_ids[None, :]
    )
    grads = grads + jnp.sum(
        jnp.where(global_hits[:, :, None, None], global_total[:, None], 0.0), axis=0
    )
    random_terms = terms[:, 3 + GLOB :].reshape(entry_count, BLOCK * 2 * DH).astype(jnp.bfloat16)
    outgoing = jnp.dot(
        placing.astype(jnp.bfloat16), random_terms, preferred_element_type=jnp.float32
    ).astype(jnp.bfloat16)
    returned = lax.all_to_all(
        outgoing.reshape(seq_count, capacity, BLOCK, 2 * DH),
        "seq",
        split_axis=0,
        concat_axis=0,
        tiled=True,
    )
    landing = (incoming[None, :] == block_ids[:, None]).astype(jnp.bfloat16)
    grads = grads + jnp.dot(
        landing,
        returned.reshape(position_count, BLOCK * 2 * DH),
        preferred_element_type=jnp.float32,
    ).reshape(blocks_here, BLOCK, 2 * DH)
    packed = grads.astype(jnp.bfloat16).reshape(tok_count, 1, 2 * DH)
    restored = lax.all_to_all(packed, "head", split_axis=0, concat_axis=1, tiled=True)
    d_keys = restored[:, :, :DH].reshape(short, KVH * DH)
    d_values = restored[:, :, DH:].reshape(short, KVH * DH)
    return (attn_out, d_queries, d_keys, d_values)


def solution(mesh):
    in_specs = (
        P("seq", "head"),
        P(("seq", "head"), None),
        P(("seq", "head"), None),
        P("seq", "head"),
        P("seq", None),
        P(),
    )
    out_specs = (
        P("seq", "head"),
        P("seq", "head"),
        P(("seq", "head"), None),
        P(("seq", "head"), None),
    )
    return jax.shard_map(body, mesh=mesh, in_specs=in_specs, out_specs=out_specs, check_vma=False)
```

profile of v0, /device:TPU:1, one launch (start us, length us, event | category | flops | bytes accessed | tf_op | source)
XLA Modules:
  0.0 672.8 jit_solution(9760338004758471083)
XLA Ops:
  7.2 0.8 reshape.390
  8.3 0.8 copy.90
  9.0 18.4 %all-to-all-start.1 = ((s32[128,1,1]{2,1,0:T(1,128)}), s32[128,1,1]{2,1,0:T(1,128)S(1)}, u32[]{:S(2)}, u32[]{:S(2)}) async-start(s32[128,1,1]{2,1,0:T(1,128)} %copy.90), calls=%async_computation.1 | async-start | bytes 131072 | tf_op jit(solution)/shard_map/all_to_all | solution.py:86
  27.4 0.9 copy_bitcast_fusion.7
  28.3 0.7 pad_maximum_fusion.3
  29.0 9.9 %all-to-all-done.1 = s32[128,1,1]{2,1,0:T(1,128)S(1)} async-done(((s32[128,1,1]{2,1,0:T(1,128)}), s32[128,1,1]{2,1,0:T(1,128)S(1)}, u32[]{:S(2)}, u32[]{:S(2)}) %all-to-all-start.1) | async-done | bytes 544 | tf_op jit(solution)/shard_map/all_to_all | solution.py:86
  38.9 4.0 all-to-all-start
  42.9 2.3 reduce
  45.2 2.5 all-to-all-done
  47.7 2.8 gather_fusion.2
  50.5 8.4 %all-to-all-start.2 = ((bf16[128,1,64,256]{3,2,1,0:T(8,128)(2,1)}), bf16[128,1,64,256]{3,2,1,0:T(8,128)(2,1)}, u32[]{:S(2)}, u32[]{:S(2)}) async-start(bf16[128,1,64,256]{3,2,1,0:T(8,128)(2,1)} %bitcast.301), calls=%async_computation.2 | async-start | bytes 8388608 | tf_op jit(solution)/shard_map/all_to_all | solution.py:90
  59.0 0.6 fusion.58
  65.6 3.5 collective-permute-start
  69.2 2.1 collective-permute-start.1
  71.3 0.6 select_bitcast_fusion.1
  72.0 72.9 %collective-permute-done = bf16[64,256]{1,0:T(8,128)(2,1)S(1)} collective-permute-done((bf16[64,256]{1,0:T(8,128)(2,1)S(1)}, bf16[64,256]{1,0:T(8,128)(2,1)S(1)}, u32[]{:S(2)}, u32[]{:S(2)}) %collective-permute-start) | collective-permute-done | bytes 32800 | tf_op jit(solution)/shard_map/ppermute | solution.py:22
  144.8 7.2 %collective-permute-done.1 = bf16[64,256]{1,0:T(8,128)(2,1)S(1)} collective-permute-done((bf16[64,256]{1,0:T(8,128)(2,1)S(1)}, bf16[64,256]{1,0:T(8,128)(2,1)S(1)}, u32[]{:S(2)}, u32[]{:S(2)}) %collective-permute-start.1) | collective-permute-done | bytes 32800 | tf_op jit(solution)/shard_map/ppermute | solution.py:24
  152.1 164.7 %all-reduce.10.cloned.1.call-done = (bf16[1,64,256]{2,1,0:T(8,128)(2,1)}, bf16[1,64,256]{2,1,0:T(8,128)(2,1)}) async-done(((bf16[1,64,256]{2,1,0:T(8,128)(2,1)}, bf16[1,64,256]{2,1,0:T(8,128)(2,1)}), (bf16[1,64,256]{2,1,0:T(8,128)(2,1)}, bf16[1,64,256]{2,1,0:T(8,128)(2,1)})) %all-reduce.10.cloned.1.call-update) | async-done | bytes 65552 | tf_op jit(solution)/shard_map/psum | solution.py:33
  316.8 3.9 pad_maximum_fusion.1
  320.6 18.4 %while.24 = (s32[]{:T(128)}, bf16[4,64,8,128]{3,1,2,0:T(8,128)(2,1)S(1)}, f32[4,8,64,1]{2,1,3,0:T(8,128)S(1)}, s32[4,13]{1,0:T(4,128)S(1)}, bf16[136,64,256]{2,1...) while((s32[]{:T(128)}, ...), condition=%wide.region_7.8_spmd, body=%wide.region_4.7_spmd.sunk | while | flops 221151776 | bytes 6817576 | solution.py:124
  320.8 2.8 gather_fusion
  324.7 0.5 fusion.83
  325.4 2.8 gather_fusion
  329.3 0.5 fusion.83
  330.0 2.8 gather_fusion
  334.6 2.8 gather_fusion
  339.0 29.0 %while.25 = (s32[]{:T(128)}, bf16[4,64,8,128]{3,2,1,0:T(8,128)(2,1)}, f32[4,13,64,256]{3,2,1,0:T(8,128)}, s32[4,13]{1,0:T(4,128)S(1)}, bf16[136,64,256]{2,1,0:T(...) while((s32[]{:T(128)}, ...), condition=%wide.region_10.11_spmd, body=%wide.region_8.10_spmd.sunk | while | flops 548954624 | bytes 15144784 | solution.py:156
  339.4 2.8 gather_fusion.1
  344.6 0.8 copy_dynamic-update-slice_fusion.2
  345.3 1.0 constant_dynamic-update-slice_fusion.2
  346.7 2.8 gather_fusion.1
  351.9 0.8 copy_dynamic-update-slice_fusion.2
  352.6 1.0 constant_dynamic-update-slice_fusion.2
  354.0 2.8 gather_fusion.1
  359.1 0.8 copy_dynamic-update-slice_fusion.2
  359.9 1.0 constant_dynamic-update-slice_fusion.2
  361.2 2.8 gather_fusion.1
  366.3 0.8 copy_dynamic-update-slice_fusion.2
  367.1 1.0 constant_dynamic-update-slice_fusion.2
  368.0 2.4 convert.16
  370.6 0.6 copy.124
  371.2 1.4 convolution_convert_fusion.1
  372.5 3.2 copy.125
  375.8 6.8 %all-to-all-start.3 = ((bf16[128,1,64,256]{3,2,1,0:T(8,128)(2,1)}), bf16[128,1,64,256]{3,2,1,0:T(8,128)(2,1)}, u32[]{:S(2)}, u32[]{:S(2)}) async-start(bf16[128,1,64,256]{3,2,1,0:T(8,128)(2,1)} %bitcast.302), calls=%async_computation.3 | async-start | bytes 8388608 | tf_op jit(solution)/shard_map/all_to_all | solution.py:193
  382.7 4.0 copy.97
  386.7 0.7 slice_reduce_fusion
  387.4 0.8 slice_bitcast_fusion.16
  388.2 3.2 collective-permute-start.2
  391.4 2.1 collective-permute-start.3
  393.6 1.1 slice_bitcast_fusion.11
  394.7 74.3 %collective-permute-done.2 = bf16[64,256]{1,0:T(8,128)(2,1)S(1)} collective-permute-done((bf16[64,256]{1,0:T(8,128)(2,1)S(1)}, bf16[64,256]{1,0:T(8,128)(2,1)S(1)}, u32[]{:S(2)}, u32[]{:S(2)}) %collective-permute-start.2) | collective-permute-done | bytes 32800 | tf_op jit(solution)/shard_map/ppermute | solution.py:22
  469.0 6.2 collective-permute-done.3
  475.3 166.2 %all-reduce.8.cloned.1.call-done = f32[2,64,256]{2,1,0:T(8,128)} async-done(((f32[2,64,256]{2,1,0:T(8,128)}), f32[2,64,256]{2,1,0:T(8,128)}) %all-reduce.8.cloned.1.call-update) | async-done | bytes 131088 | tf_op jit(solution)/shard_map/psum | solution.py:182
  641.5 1.0 select_reduce_fusion
  642.5 6.9 %copy.109 = bf16[128,1,64,256]{0,3,2,1:T(8,128)(2,1)} copy(bf16[128,1,64,256]{3,2,1,0:T(8,128)(2,1)} %all-to-all-done.3) | data formatting | bytes 8388608 | tf_op jit(solution)/shard_map/reshape | solution.py:203
  649.5 3.5 fusion.35
  653.5 0.7 reduce.2
  654.2 0.7 reshape.443
  654.9 4.0 all-to-all-start.4
  659.2 0.9 copy.139
  660.1 0.9 copy.140
  661.0 3.5 all-to-all-done.4
  664.6 0.6 copy.141
  665.3 0.6 copy.142
  (155 shorter events, 18.7 us)
Async XLA Ops:
  7.2 20.3 %copy-start = (bf16[64,512]{1,0:T(8,128)(2,1)S(1)}, bf16[64,512]{1,0:T(8,128)(2,1)}, u32[]{:S(2)}) copy-start(bf16[64,512]{1,0:T(8,128)(2,1)} %param.11) | copy-start | bytes 196612
  9.0 29.8 %all-to-all-start.1 = ((s32[128,1,1]{2,1,0:T(1,128)}), s32[128,1,1]{2,1,0:T(1,128)S(1)}, u32[]{:S(2)}, u32[]{:S(2)}) async-start(s32[128,1,1]{2,1,0:T(1,128)} %copy.90), calls=%async_computation.1 | async-start | bytes 131072 | tf_op jit(solution)/shard_map/all_to_all | solution.py:86
  38.9 8.8 %all-to-all-start = ((bf16[64,4,256]{2,0,1:T(8,128)(2,1)}), bf16[64,4,256]{2,0,1:T(8,128)(2,1)S(1)}, u32[]{:S(2)}, u32[]{:S(2)}) async-start(bf16[64,4,256]{2,0,1:T(8,128)(2,1)} %pad_maximum_fusion.3), calls=%async_computation | async-start | bytes 262144 | tf_op jit(solution)/shard_map/all_to_all | solution.py:59
  50.5 8.5 %copy-start.9 = (s32[2]{0:T(128)S(1)}, s32[2]{0:T(128)}, u32[]{:S(2)}) copy-start(s32[2]{0:T(128)} %param.15) | copy-start | bytes 28
  50.5 14.6 %copy-start.5 = (bf16[256,1024]{1,0:T(8,128)(2,1)S(1)}, bf16[256,1024]{1,0:T(8,128)(2,1)}, u32[]{:S(2)}) copy-start(bf16[256,1024]{1,0:T(8,128)(2,1)} %param.10) | copy-start | bytes 1572868
  50.5 14.8 %copy-start.6 = (bf16[256,1024]{1,0:T(8,128)(2,1)S(1)}, bf16[256,1024]{1,0:T(8,128)(2,1)}, u32[]{:S(2)}) copy-start(bf16[256,1024]{1,0:T(8,128)(2,1)} %param.13) | copy-start | bytes 1572868
  50.5 14.9 %copy-start.8 = (s32[4,8]{1,0:T(4,128)S(1)}, s32[4,8]{1,0:T(4,128)}, u32[]{:S(2)}) copy-start(s32[4,8]{1,0:T(4,128)} %param.14) | copy-start | bytes 388
  50.5 266.3 %all-to-all-start.2 = ((bf16[128,1,64,256]{3,2,1,0:T(8,128)(2,1)}), bf16[128,1,64,256]{3,2,1,0:T(8,128)(2,1)}, u32[]{:S(2)}, u32[]{:S(2)}) async-start(bf16[128,1,64,256]{3,2,1,0:T(8,128)(2,1)} %bitcast.301), calls=%async_computation.2 | async-start | bytes 8388608 | tf_op jit(solution)/shard_map/all_to_all | solution.py:90
  58.9 257.8 %all-reduce.10.cloned.1.call-start = ((), (), s32[]{:S(2)}) async-start(), calls=%async_computation.6 | async-start | bytes 131072 | tf_op jit(solution)/shard_map/psum | solution.py:33
  65.6 79.2 %collective-permute-start = (bf16[64,256]{1,0:T(8,128)(2,1)S(1)}, bf16[64,256]{1,0:T(8,128)(2,1)S(1)}, u32[]{:S(2)}, u32[]{:S(2)}) collective-permute-start(bf16[64,256]{1,0:T(8,128)(2,1)S(1)} %get-tuple-element.230), channel_id=1, source_target_pairs={{0,4},{4,8},{8,12},{12,16},{16,20},{20,24},{24,28},{28,32},{32,36}... | collective-permute-start | bytes 98312 | tf_op jit(solution)/shard_map/ppermute | solution.py:22
  69.2 82.9 %collective-permute-start.1 = (bf16[64,256]{1,0:T(8,128)(2,1)S(1)}, bf16[64,256]{1,0:T(8,128)(2,1)S(1)}, u32[]{:S(2)}, u32[]{:S(2)}) collective-permute-start(bf16[64,256]{1,0:T(8,128)(2,1)S(1)} %get-tuple-element.231), channel_id=1, source_target_pairs={{4,0},{8,4},{12,8},{16,12},{20,16},{24,20},{28,24},{32,28},{36,32}... | collective-permute-start | bytes 98312 | tf_op jit(solution)/shard_map/ppermute | solution.py:24
  368.0 2.5 copy-start.3
  370.4 2.1 copy-start.2
  375.8 6.9 %copy-start.1 = (f32[4,13,64,256]{3,2,1,0:T(8,128)S(1)}, f32[4,13,64,256]{3,2,1,0:T(8,128)}, u32[]{:S(2)}) copy-start(f32[4,13,64,256]{3,2,1,0:T(8,128)} %get-tuple-element.98) | copy-start | bytes 10223620
  375.8 266.8 %all-to-all-start.3 = ((bf16[128,1,64,256]{3,2,1,0:T(8,128)(2,1)}), bf16[128,1,64,256]{3,2,1,0:T(8,128)(2,1)}, u32[]{:S(2)}, u32[]{:S(2)}) async-start(bf16[128,1,64,256]{3,2,1,0:T(8,128)(2,1)} %bitcast.302), calls=%async_computation.3 | async-start | bytes 8388608 | tf_op jit(solution)/shard_map/all_to_all | solution.py:193
  382.5 258.9 %all-reduce.8.cloned.1.call-start = ((), (), s32[]{:S(2)}) async-start(), calls=%async_computation.5 | async-start | bytes 262144 | tf_op jit(solution)/shard_map/psum | solution.py:182
  388.2 80.8 %collective-permute-start.2 = (bf16[64,256]{1,0:T(8,128)(2,1)S(1)}, bf16[64,256]{1,0:T(8,128)(2,1)S(1)}, u32[]{:S(2)}, u32[]{:S(2)}) collective-permute-start(bf16[64,256]{1,0:T(8,128)(2,1)S(1)} %get-tuple-element.226), channel_id=1, source_target_pairs={{0,4},{4,8},{8,12},{12,16},{16,20},{20,24},{24,28},{28,32},{32,36}... | collective-permute-start | bytes 98312 | tf_op jit(solution)/shard_map/ppermute | solution.py:22
  391.4 83.8 %collective-permute-start.3 = (bf16[64,256]{1,0:T(8,128)(2,1)S(1)}, bf16[64,256]{1,0:T(8,128)(2,1)S(1)}, u32[]{:S(2)}, u32[]{:S(2)}) collective-permute-start(bf16[64,256]{1,0:T(8,128)(2,1)S(1)} %get-tuple-element.227), channel_id=1, source_target_pairs={{4,0},{8,4},{12,8},{16,12},{20,16},{24,20},{28,24},{32,28},{36,32}... | collective-permute-start | bytes 98312 | tf_op jit(solution)/shard_map/ppermute | solution.py:24
  649.4 9.4 %copy-start.4 = (bf16[4,64,8,128]{3,1,2,0:T(8,128)(2,1)S(1)}, bf16[4,64,8,128]{3,1,2,0:T(8,128)(2,1)}, u32[]{:S(2)}) copy-start(bf16[4,64,8,128]{3,1,2,0:T(8,128)(2,1)} %copy-done.3) | copy-start | bytes 1572868
  649.5 9.7 %copy-start.7 = (bf16[4,64,8,128]{3,2,1,0:T(8,128)(2,1)S(1)}, bf16[4,64,8,128]{3,2,1,0:T(8,128)(2,1)}, u32[]{:S(2)}) copy-start(bf16[4,64,8,128]{3,2,1,0:T(8,128)(2,1)} %get-tuple-element.97) | copy-start | bytes 1572868
  654.9 9.6 %all-to-all-start.4 = ((bf16[4,2,8192]{2,1,0:T(2,128)(2,1)}), bf16[4,2,8192]{2,1,0:T(2,128)(2,1)S(1)}, u32[]{:S(2)}, u32[]{:S(2)}) async-start(bf16[4,2,8192]{2,1,0:T(2,128)(2,1)} %reshape.443), calls=%async_computation.4 | async-start | bytes 262144 | tf_op jit(solution)/shard_map/all_to_all | solution.py:207
Sparse Core Ops, SparseCore 0:
  72.1 244.6 all-reduce.9
  387.5 253.9 all-reduce.7
where the time goes:
time: 674 us; the launch traced here: 673 us
  waiting for transfers between devices  507 us (75%)
  local copies, waits for them, and re-layouts  59.1 us (9%)
  starting transfers between devices  52.7 us (8%)
  between operations  19.6 us (3%)
  matrix products  17.9 us (3%)
  other arithmetic  15.6 us (2%)
    psum x1, waiting for transfers between devices, body(): global_total = lax.psum(global_terms, 'seq')  166 us
    psum x1, waiting for transfers between devices, broadcast(): return lax.psum(block, axis)  165 us
    ppermute x2, waiting for transfers between devices, padded_2(): lax.ppermute(tail, axis, [(i, (i + 1) % count) for i in range(ends)])  147 us
    gather x8, local copies, waits for them, and re-layouts, key_rows(): chosen = library[spots]  22.7 us
    all_to_all x1, starting transfers between devices, body(): lax.all_to_all(wanted, 'seq', split_axis=0, concat_axis=0, tiled=True)  18.4 us
  transfers between devices with their start and end apart: 11, of which 9 were waited for; matrix products, arithmetic and copies ran while one was open for 2% of the time, Pallas kernels for 0%

commit v1 on v0

--- a/solution.py
+++ b/solution.py
@@ -179,7 +179,8 @@
     )
     grads = grads + edge_first + edge_last
     global_terms = jnp.sum(terms[:, 3 : 3 + GLOB], axis=0)
-    global_total = lax.psum(global_terms, "seq")
+    pieces = lax.all_gather(global_terms, "seq", axis=0, tiled=False)
+    global_total = pieces.sum(axis=0)
     global_hits = ((glob_blocks // blocks_here)[:, None] == here) & (
         (glob_blocks % blocks_here)[:, None] == block_ids[None, :]
     )

time: 674 us -> 580 us (0.86)
  waiting for transfers between devices: 507 us -> 409 us
  other arithmetic: 15.6 us -> 22.5 us
    psum x1 -> x0, waiting for transfers between devices: 166 us -> none  [body(): global_total = lax.psum(global_terms, 'seq')]
    all_gather x0 -> x1, waiting for transfers between devices: none -> 57.6 us  [body(): pieces = lax.all_gather(global_terms, 'seq', axis=0, tiled=False)]
    ppermute x2, waiting for transfers between devices: 147 us -> 155 us  [padded_2(): lax.ppermute(tail, axis, [(i, (i + 1) % count) for i in range(ends)])]
    reduce_sum x0 -> x1, other arithmetic: none -> 6.82 us  [body(): global_total = pieces.sum(axis=0)]
  transfers between devices with their start and end apart: 11 -> 11, of which waited for: 9 -> 10; matrix products, arithmetic and copies ran while one was open for 2% -> 4% of each run, Pallas kernels for 0% -> 0%
where the time goes in v1:
time: 580 us; the launch traced here: 578 us
  waiting for transfers between devices  409 us (71%)
  local copies, waits for them, and re-layouts  56.4 us (10%)
  starting transfers between devices  52.7 us (9%)
  other arithmetic  22.5 us (4%)
  between operations  19.6 us (3%)
  matrix products  17.9 us (3%)
    psum x1, waiting for transfers between devices, broadcast(): return lax.psum(block, axis)  165 us
    ppermute x2, waiting for transfers between devices, padded_2(): lax.ppermute(tail, axis, [(i, (i + 1) % count) for i in range(ends)])  155 us
    all_gather x1, waiting for transfers between devices, body(): pieces = lax.all_gather(global_terms, 'seq', axis=0, tiled=False)  57.6 us
    gather x8, local copies, waits for them, and re-layouts, key_rows(): chosen = library[spots]  22.7 us
    all_to_all x1, starting transfers between devices, body(): lax.all_to_all(wanted, 'seq', split_axis=0, concat_axis=0, tiled=True)  18.4 us
    ppermute x2, waiting for transfers between devices, padded_2(): lax.ppermute(head, axis, [((i + 1) % count, i) for i in range(ends)])  11.8 us
  transfers between devices with their start and end apart: 11, of which 10 were waited for; matrix products, arithmetic and copies ran while one was open for 4% of the time, Pallas kernels for 0%

profile of v1, /device:TPU:1, one launch (start us, length us, event | category | flops | bytes accessed | tf_op | source)
XLA Modules:
  0.0 578.3 jit_solution(6696569952455034976)
XLA Ops:
  7.2 0.8 reshape.390
  8.3 0.8 copy.90
  9.0 18.4 %all-to-all-start.1 = ((s32[128,1,1]{2,1,0:T(1,128)}), s32[128,1,1]{2,1,0:T(1,128)S(1)}, u32[]{:S(2)}, u32[]{:S(2)}) async-start(s32[128,1,1]{2,1,0:T(1,128)} %copy.90), calls=%async_computation.1 | async-start | bytes 131072 | tf_op jit(solution)/shard_map/all_to_all | solution.py:86
  27.5 0.9 copy_bitcast_fusion.7
  28.3 0.7 pad_maximum_fusion.3
  29.0 9.9 %all-to-all-done.1 = s32[128,1,1]{2,1,0:T(1,128)S(1)} async-done(((s32[128,1,1]{2,1,0:T(1,128)}), s32[128,1,1]{2,1,0:T(1,128)S(1)}, u32[]{:S(2)}, u32[]{:S(2)}) %all-to-all-start.1) | async-done | bytes 544 | tf_op jit(solution)/shard_map/all_to_all | solution.py:86
  38.9 4.0 all-to-all-start
  42.9 2.3 reduce
  45.2 2.5 all-to-all-done
  47.7 2.8 gather_fusion.2
  50.5 8.4 %all-to-all-start.2 = ((bf16[128,1,64,256]{3,2,1,0:T(8,128)(2,1)}), bf16[128,1,64,256]{3,2,1,0:T(8,128)(2,1)}, u32[]{:S(2)}, u32[]{:S(2)}) async-start(bf16[128,1,64,256]{3,2,1,0:T(8,128)(2,1)} %bitcast.303), calls=%async_computation.2 | async-start | bytes 8388608 | tf_op jit(solution)/shard_map/all_to_all | solution.py:90
  59.0 0.6 fusion.58
  65.7 3.5 collective-permute-start
  69.2 1.9 collective-permute-start.1
  71.1 0.6 select_bitcast_fusion.1
  72.0 72.8 %collective-permute-done = bf16[64,256]{1,0:T(8,128)(2,1)S(1)} collective-permute-done((bf16[64,256]{1,0:T(8,128)(2,1)S(1)}, bf16[64,256]{1,0:T(8,128)(2,1)S(1)}, u32[]{:S(2)}, u32[]{:S(2)}) %collective-permute-start) | collective-permute-done | bytes 32800 | tf_op jit(solution)/shard_map/ppermute | solution.py:22
  144.9 7.2 %collective-permute-done.1 = bf16[64,256]{1,0:T(8,128)(2,1)S(1)} collective-permute-done((bf16[64,256]{1,0:T(8,128)(2,1)S(1)}, bf16[64,256]{1,0:T(8,128)(2,1)S(1)}, u32[]{:S(2)}, u32[]{:S(2)}) %collective-permute-start.1) | collective-permute-done | bytes 32800 | tf_op jit(solution)/shard_map/ppermute | solution.py:24
  152.1 165.0 %all-reduce.7.cloned.1.call-done = (bf16[1,64,256]{2,1,0:T(8,128)(2,1)}, bf16[1,64,256]{2,1,0:T(8,128)(2,1)}) async-done(((bf16[1,64,256]{2,1,0:T(8,128)(2,1)}, bf16[1,64,256]{2,1,0:T(8,128)(2,1)}), (bf16[1,64,256]{2,1,0:T(8,128)(2,1)}, bf16[1,64,256]{2,1,0:T(8,128)(2,1)})) %all-reduce.7.cloned.1.call-update) | async-done | bytes 65552 | tf_op jit(solution)/shard_map/psum | solution.py:33
  317.1 3.9 pad_maximum_fusion.1
  321.0 18.4 %while.24 = (s32[]{:T(128)}, bf16[4,64,8,128]{3,1,2,0:T(8,128)(2,1)S(1)}, f32[4,8,64,1]{2,1,3,0:T(8,128)S(1)}, s32[4,13]{1,0:T(4,128)S(1)}, bf16[136,64,256]{2,1...) while((s32[]{:T(128)}, ...), condition=%wide.region_7.8_spmd, body=%wide.region_4.7_spmd.sunk | while | flops 221151776 | bytes 6817576 | solution.py:124
  321.2 2.8 gather_fusion
  325.0 0.5 fusion.83
  325.8 2.8 gather_fusion
  329.6 0.5 fusion.83
  330.4 2.8 gather_fusion
  335.0 2.8 gather_fusion
  339.4 29.0 %while.25 = (s32[]{:T(128)}, bf16[4,64,8,128]{3,2,1,0:T(8,128)(2,1)}, f32[4,13,64,256]{3,2,1,0:T(8,128)}, s32[4,13]{1,0:T(4,128)S(1)}, bf16[136,64,256]{2,1,0:T(...) while((s32[]{:T(128)}, ...), condition=%wide.region_10.11_spmd, body=%wide.region_8.10_spmd.sunk | while | flops 548954624 | bytes 15144784 | solution.py:156
  339.8 2.8 gather_fusion.1
  344.9 0.8 copy_dynamic-update-slice_fusion.2
  345.7 1.0 constant_dynamic-update-slice_fusion.2
  347.1 2.8 gather_fusion.1
  352.2 0.8 copy_dynamic-update-slice_fusion.2
  353.0 1.0 constant_dynamic-update-slice_fusion.2
  354.3 2.8 gather_fusion.1
  359.4 0.8 copy_dynamic-update-slice_fusion.2
  360.2 1.0 constant_dynamic-update-slice_fusion.2
  361.5 2.8 gather_fusion.1
  366.7 0.8 copy_dynamic-update-slice_fusion.2
  367.4 0.9 constant_dynamic-update-slice_fusion.2
  368.4 1.9 slice_reduce_fusion
  370.3 2.2 convert.16
  372.7 0.6 copy.124
  373.2 1.4 convolution_convert_fusion.1
  374.6 3.2 copy.125
  377.8 6.8 %all-to-all-start.3 = ((bf16[128,1,64,256]{3,2,1,0:T(8,128)(2,1)}), bf16[128,1,64,256]{3,2,1,0:T(8,128)(2,1)}, u32[]{:S(2)}, u32[]{:S(2)}) async-start(bf16[128,1,64,256]{3,2,1,0:T(8,128)(2,1)} %bitcast.304), calls=%async_computation.3 | async-start | bytes 8388608 | tf_op jit(solution)/shard_map/all_to_all | solution.py:194
  384.7 2.2 copy.97
  387.0 0.9 slice_bitcast_fusion.16
  387.8 3.2 collective-permute-start.2
  391.0 2.1 collective-permute-start.3
  393.3 82.1 %collective-permute-done.2 = bf16[64,256]{1,0:T(8,128)(2,1)S(1)} collective-permute-done((bf16[64,256]{1,0:T(8,128)(2,1)S(1)}, bf16[64,256]{1,0:T(8,128)(2,1)S(1)}, u32[]{:S(2)}, u32[]{:S(2)}) %collective-permute-start.2) | collective-permute-done | bytes 32800 | tf_op jit(solution)/shard_map/ppermute | solution.py:22
  475.5 4.6 collective-permute-done.3
  480.2 4.1 all-to-all-done.3
  484.4 6.9 %copy.109 = bf16[128,1,64,256]{0,3,2,1:T(8,128)(2,1)} copy(bf16[128,1,64,256]{3,2,1,0:T(8,128)(2,1)} %all-to-all-done.3) | data formatting | bytes 8388608 | tf_op jit(solution)/shard_map/reshape | solution.py:204
  491.3 57.6 %all-gather.3.cloned.1.call-done = f32[256,64,256]{2,1,0:T(8,128)} async-done(((f32[2,64,256]{2,1,0:T(8,128)}), f32[256,64,256]{2,1,0:T(8,128)}) %all-gather.3.cloned.1.call-update) | async-done | bytes 16777232 | tf_op jit(solution)/shard_map/all_gather | solution.py:182
  548.9 6.8 %reduce_sum.69 = f32[2,64,256]{2,1,0:T(8,128)S(1)} reduce(f32[128,2,64,256]{3,2,1,0:T(8,128)} %bitcast.302, f32[]{:T(128)} %constant.151.clone.1), dimensions={0}, to_apply=%region_12.13 | reduce | flops 4161536 | bytes 16908292 | tf_op jit(solution)/shard_map/reduce_sum | solution.py:183
  555.8 3.5 fusion.35
  559.9 0.7 reduce.2
  560.5 0.7 reshape.444
  561.2 4.0 all-to-all-start.4
  565.6 0.9 copy.139
  566.4 0.9 copy.140
  567.3 2.7 all-to-all-done.4
  570.2 0.6 copy.141
  570.9 0.6 copy.142
  (160 shorter events, 19.1 us)
Async XLA Ops:
  7.2 20.3 %copy-start = (bf16[64,512]{1,0:T(8,128)(2,1)S(1)}, bf16[64,512]{1,0:T(8,128)(2,1)}, u32[]{:S(2)}) copy-start(bf16[64,512]{1,0:T(8,128)(2,1)} %param.11) | copy-start | bytes 196612
  9.0 29.8 %all-to-all-start.1 = ((s32[128,1,1]{2,1,0:T(1,128)}), s32[128,1,1]{2,1,0:T(1,128)S(1)}, u32[]{:S(2)}, u32[]{:S(2)}) async-start(s32[128,1,1]{2,1,0:T(1,128)} %copy.90), calls=%async_computation.1 | async-start | bytes 131072 | tf_op jit(solution)/shard_map/all_to_all | solution.py:86
  38.9 8.8 %all-to-all-start = ((bf16[64,4,256]{2,0,1:T(8,128)(2,1)}), bf16[64,4,256]{2,0,1:T(8,128)(2,1)S(1)}, u32[]{:S(2)}, u32[]{:S(2)}) async-start(bf16[64,4,256]{2,0,1:T(8,128)(2,1)} %pad_maximum_fusion.3), calls=%async_computation | async-start | bytes 262144 | tf_op jit(solution)/shard_map/all_to_all | solution.py:59
  50.5 8.5 %copy-start.11 = (s32[2]{0:T(128)S(1)}, s32[2]{0:T(128)}, u32[]{:S(2)}) copy-start(s32[2]{0:T(128)} %param.15) | copy-start | bytes 28
  50.5 14.6 %copy-start.7 = (bf16[256,1024]{1,0:T(8,128)(2,1)S(1)}, bf16[256,1024]{1,0:T(8,128)(2,1)}, u32[]{:S(2)}) copy-start(bf16[256,1024]{1,0:T(8,128)(2,1)} %param.10) | copy-start | bytes 1572868
  50.5 14.8 %copy-start.8 = (bf16[256,1024]{1,0:T(8,128)(2,1)S(1)}, bf16[256,1024]{1,0:T(8,128)(2,1)}, u32[]{:S(2)}) copy-start(bf16[256,1024]{1,0:T(8,128)(2,1)} %param.13) | copy-start | bytes 1572868
  50.5 14.9 %copy-start.10 = (s32[4,8]{1,0:T(4,128)S(1)}, s32[4,8]{1,0:T(4,128)}, u32[]{:S(2)}) copy-start(s32[4,8]{1,0:T(4,128)} %param.14) | copy-start | bytes 388
  50.5 266.6 %all-to-all-start.2 = ((bf16[128,1,64,256]{3,2,1,0:T(8,128)(2,1)}), bf16[128,1,64,256]{3,2,1,0:T(8,128)(2,1)}, u32[]{:S(2)}, u32[]{:S(2)}) async-start(bf16[128,1,64,256]{3,2,1,0:T(8,128)(2,1)} %bitcast.303), calls=%async_computation.2 | async-start | bytes 8388608 | tf_op jit(solution)/shard_map/all_to_all | solution.py:90
  58.9 258.2 %all-reduce.7.cloned.1.call-start = ((), (), s32[]{:S(2)}) async-start(), calls=%async_computation.6 | async-start | bytes 131072 | tf_op jit(solution)/shard_map/psum | solution.py:33
  65.7 79.2 %collective-permute-start = (bf16[64,256]{1,0:T(8,128)(2,1)S(1)}, bf16[64,256]{1,0:T(8,128)(2,1)S(1)}, u32[]{:S(2)}, u32[]{:S(2)}) collective-permute-start(bf16[64,256]{1,0:T(8,128)(2,1)S(1)} %get-tuple-element.230), channel_id=1, source_target_pairs={{0,4},{4,8},{8,12},{12,16},{16,20},{20,24},{24,28},{28,32},{32,36}... | collective-permute-start | bytes 98312 | tf_op jit(solution)/shard_map/ppermute | solution.py:22
  69.2 82.9 %collective-permute-start.1 = (bf16[64,256]{1,0:T(8,128)(2,1)S(1)}, bf16[64,256]{1,0:T(8,128)(2,1)S(1)}, u32[]{:S(2)}, u32[]{:S(2)}) collective-permute-start(bf16[64,256]{1,0:T(8,128)(2,1)S(1)} %get-tuple-element.231), channel_id=1, source_target_pairs={{4,0},{8,4},{12,8},{16,12},{20,16},{24,20},{28,24},{32,28},{36,32}... | collective-permute-start | bytes 98312 | tf_op jit(solution)/shard_map/ppermute | solution.py:24
  71.8 477.1 %all-gather.3.cloned.1.call-start = ((), (), s32[]{:S(2)}) async-start(), calls=%async_computation.5 | async-start | bytes 16908288 | tf_op jit(solution)/shard_map/all_gather | solution.py:182
  368.4 4.3 copy-start.5
  372.5 2.1 copy-start.4
  377.8 6.9 %copy-start.2 = (f32[4,13,64,256]{3,2,1,0:T(8,128)S(1)}, f32[4,13,64,256]{3,2,1,0:T(8,128)}, u32[]{:S(2)}) copy-start(f32[4,13,64,256]{3,2,1,0:T(8,128)} %get-tuple-element.98) | copy-start | bytes 10223620
  377.8 106.5 %all-to-all-start.3 = ((bf16[128,1,64,256]{3,2,1,0:T(8,128)(2,1)}), bf16[128,1,64,256]{3,2,1,0:T(8,128)(2,1)}, u32[]{:S(2)}, u32[]{:S(2)}) async-start(bf16[128,1,64,256]{3,2,1,0:T(8,128)(2,1)} %bitcast.304), calls=%async_computation.3 | async-start | bytes 8388608 | tf_op jit(solution)/shard_map/all_to_all | solution.py:194
  387.0 6.2 %copy-start.3 = (f32[4,13,64,256]{3,0,2,1:T(4,128)}, f32[4,13,64,256]{3,0,2,1:T(4,128)S(1)}, u32[]{:S(2)}) copy-start(f32[4,13,64,256]{3,0,2,1:T(4,128)S(1)} %copy.97) | copy-start | bytes 10223620
  387.8 87.6 %collective-permute-start.2 = (bf16[64,256]{1,0:T(8,128)(2,1)S(1)}, bf16[64,256]{1,0:T(8,128)(2,1)S(1)}, u32[]{:S(2)}, u32[]{:S(2)}) collective-permute-start(bf16[64,256]{1,0:T(8,128)(2,1)S(1)} %get-tuple-element.226), channel_id=1, source_target_pairs={{0,4},{4,8},{8,12},{12,16},{16,20},{20,24},{24,28},{28,32},{32,36}... | collective-permute-start | bytes 98312 | tf_op jit(solution)/shard_map/ppermute | solution.py:22
  391.0 89.1 %collective-permute-start.3 = (bf16[64,256]{1,0:T(8,128)(2,1)S(1)}, bf16[64,256]{1,0:T(8,128)(2,1)S(1)}, u32[]{:S(2)}, u32[]{:S(2)}) collective-permute-start(bf16[64,256]{1,0:T(8,128)(2,1)S(1)} %get-tuple-element.227), channel_id=1, source_target_pairs={{4,0},{8,4},{12,8},{16,12},{20,16},{24,20},{28,24},{32,28},{36,32}... | collective-permute-start | bytes 98312 | tf_op jit(solution)/shard_map/ppermute | solution.py:24
  555.7 9.5 %copy-start.6 = (bf16[4,64,8,128]{3,1,2,0:T(8,128)(2,1)S(1)}, bf16[4,64,8,128]{3,1,2,0:T(8,128)(2,1)}, u32[]{:S(2)}) copy-start(bf16[4,64,8,128]{3,1,2,0:T(8,128)(2,1)} %copy-done.5) | copy-start | bytes 1572868
  555.8 9.8 %copy-start.9 = (bf16[4,64,8,128]{3,2,1,0:T(8,128)(2,1)S(1)}, bf16[4,64,8,128]{3,2,1,0:T(8,128)(2,1)}, u32[]{:S(2)}) copy-start(bf16[4,64,8,128]{3,2,1,0:T(8,128)(2,1)} %get-tuple-element.97) | copy-start | bytes 1572868
  555.8 15.7 %copy-start.1 = (bf16[64,512]{1,0:T(8,128)(2,1)S(1)}, bf16[64,512]{1,0:T(8,128)(2,1)}, u32[]{:S(2)}) copy-start(bf16[64,512]{1,0:T(8,128)(2,1)} %param.11) | copy-start | bytes 196612
  561.2 8.8 %all-to-all-start.4 = ((bf16[4,2,8192]{2,1,0:T(2,128)(2,1)}), bf16[4,2,8192]{2,1,0:T(2,128)(2,1)S(1)}, u32[]{:S(2)}, u32[]{:S(2)}) async-start(bf16[4,2,8192]{2,1,0:T(2,128)(2,1)} %reshape.444), calls=%async_computation.4 | async-start | bytes 262144 | tf_op jit(solution)/shard_map/all_to_all | solution.py:208
Sparse Core Ops, SparseCore 0:
  71.9 245.1 all-reduce.6
  370.4 178.3 all-gather.2
